TPU v7x, 32 devices: a whole 2x2x4 slice. The times are simulated.
32 devices in a mesh: batch: 8 (over z, core), seq: 4 (over y, x).
Axes of the slice: x: 2, y: 2, z: 4, core: 2. Of those that a mesh axis runs over, the one named last changes fastest.
Arguments:
- tokens: bfloat16 [8, 2048, 768], P('batch', 'seq'), may hold values from -6 to 6
- segments: int32 [8, 2048], P('batch'), may hold values from 0 to 15, never falling along the last dimension, each value on 1 to 1280 neighbouring positions
- qkv_weight: float32 [3, 768, 768], P(None, ('batch', 'seq')), may hold values from -0.21875 to 0.21875
- qv_bias: float32 [2, 768], P(None, ('batch', 'seq')), may hold values from -1.8 to 1.8
- attn_out_weight: float32 [768, 768], P(('batch', 'seq')), may hold values from -1.75 to 1.75
- attn_out_bias: float32 [768], P(('batch', 'seq')), may hold values from -1.8 to 1.8
- norm1_gain: float32 [768], P(('batch', 'seq')), may hold values from 0.5 to 1.5
- norm1_bias: float32 [768], P(('batch', 'seq')), may hold values from -1.8 to 1.8
- up_weight: float32 [768, 3072], P(('batch', 'seq')), may hold values from -0.21875 to 0.21875
- up_bias: float32 [3072], P(('batch', 'seq')), may hold values from -1.8 to 1.8
- down_weight: float32 [3072, 768], P(('batch', 'seq')), may hold values from -0.109375 to 0.109375
- down_bias: float32 [768], P(('batch', 'seq')), may hold values from -1.8 to 1.8
- norm2_gain: float32 [768], P(('batch', 'seq')), may hold values from 0.5 to 1.5
- norm2_bias: float32 [768], P(('batch', 'seq')), may hold values from -1.8 to 1.8
- cotangent: bfloat16 [8, 2048, 768], P('batch', 'seq'), may hold values from -6 to 6
Outputs:
- output: bfloat16 [8, 2048, 768], P('batch', 'seq')
- tokens_grad: bfloat16 [8, 2048, 768], P('batch', 'seq')
- qkv_weight_grad: float32 [3, 768, 768], P(None, ('batch', 'seq'))
- qv_bias_grad: float32 [2, 768], P(None, ('batch', 'seq'))
- attn_out_weight_grad: float32 [768, 768], P(('batch', 'seq'))
- attn_out_bias_grad: float32 [768], P(('batch', 'seq'))
- norm1_gain_grad: float32 [768], P(('batch', 'seq'))
- norm1_bias_grad: float32 [768], P(('batch', 'seq'))
- up_weight_grad: float32 [768, 3072], P(('batch', 'seq'))
- up_bias_grad: float32 [3072], P(('batch', 'seq'))
- down_weight_grad: float32 [3072, 768], P(('batch', 'seq'))
- down_bias_grad: float32 [768], P(('batch', 'seq'))
- norm2_gain_grad: float32 [768], P(('batch', 'seq'))
- norm2_bias_grad: float32 [768], P(('batch', 'seq'))
Inputs may be any that keep to these rules, and one draw needn't show every extreme that they name: `segments`: along each sequence the document numbers never fall; every number appears, each as a run of 1 to 1280 tokens, one run exactly 1280.
All inputs are finite; a program needn't handle non-finite values.
Results may differ from a plain program's by a relative error of at most 0.018.
Values may be sent and summed in bfloat16 or wider, within the bound.
A program may use at most 256 MiB of HBM per device.

v0:
```python
import math

import jax
import jax.numpy as jnp
from jax import lax
from jax.sharding import PartitionSpec as P

HEAD_DIM = 64


epsilon = 1e-05
masked_score = -1e30


def layer_norm(values, gain_vec, shift_vec):
    centre = jnp.mean(values, axis=-1, keepdims=True)
    centred = values - centre
    spread = jnp.mean(centred * centred, axis=-1, keepdims=True)
    return centred * lax.rsqrt(spread + epsilon) * gain_vec + shift_vec


def gelu_exact(values):
    return jax.nn.gelu(values, approximate=False)


def split_rows(tensor, blocks, axis):
    shape = tensor.shape
    size = shape[axis] // blocks
    shaped = tensor.reshape(shape[:axis] + (blocks, size) + shape[axis + 1 :])
    return jnp.moveaxis(shaped, axis, 0)


def masked_scores(queries, query_docs, key_rows, key_docs, factor):
    scores = (
        jnp.einsum("sqhd,skhd->shqk", queries, key_rows, preferred_element_type=jnp.float32)
        * factor
    )
    same_doc = (query_docs[:, :, None] == key_docs[:, None, :])[:, None]
    return (jnp.where(same_doc, scores, masked_score), same_doc)


def absorb(running, queries, query_docs, key_rows, value_rows, key_docs, factor):
    peak_old, row_sum, context = running
    scores, same_doc = masked_scores(queries, query_docs, key_rows, key_docs, factor)
    peak_new = jnp.maximum(peak_old, jnp.max(scores, axis=-1))
    fading = jnp.exp(peak_old - peak_new)
    weights = jnp.where(same_doc, jnp.exp(scores - peak_new[..., None]), 0.0)
    row_sum = row_sum * fading + jnp.sum(weights, axis=-1)
    context = context * fading[..., None] + jnp.einsum(
        "shqk,skhd->shqd",
        weights.astype(jnp.bfloat16),
        value_rows,
        preferred_element_type=jnp.float32,
    )
    return (peak_new, row_sum, context)


def absorb_rows(running, queries, query_docs, key_rows, value_rows, key_docs):
    head_size = queries.shape[3]
    factor = head_size ** (-0.5)
    key_count = key_rows.shape[1]
    blocks = key_count // math.gcd(key_count, 512)

    def absorb_advance(state_now, element):
        return (
            absorb(state_now, queries, query_docs, element[0], element[1], element[2], factor),
            None,
        )

    running, ignored = lax.scan(
        absorb_advance,
        running,
        (
            split_rows(key_rows, blocks, 1),
            split_rows(value_rows, blocks, 1),
            split_rows(key_docs, blocks, 1),
        ),
    )
    return running


def block_grads(
    queries, query_docs, grad_context, peak_log, delta, key_rows, value_rows, key_docs, factor
):
    scores, same_doc = masked_scores(queries, query_docs, key_rows, key_docs, factor)
    probs = jnp.where(same_doc, jnp.exp(scores - peak_log[..., None]), 0.0)
    grad_probs = jnp.einsum(
        "sqhd,skhd->shqk", grad_context, value_rows, preferred_element_type=jnp.float32
    )
    grad_scores = (probs * (grad_probs - delta[..., None])).astype(jnp.bfloat16)
    part = None
    grad_keys = None
    grad_values = None
    part = (
        jnp.einsum("shqk,skhd->sqhd", grad_scores, key_rows, preferred_element_type=jnp.float32)
        * factor
    )
    grad_keys = (
        jnp.einsum("shqk,sqhd->skhd", grad_scores, queries, preferred_element_type=jnp.float32)
        * factor
    )
    grad_values = jnp.einsum(
        "shqk,sqhd->skhd",
        probs.astype(jnp.bfloat16),
        grad_context,
        preferred_element_type=jnp.float32,
    )
    return (part, grad_keys, grad_values)


def backward_rows(
    queries, query_docs, grad_context, peak_log, delta, key_rows, value_rows, key_docs
):
    seq_count, query_count, head_count, head_size = queries.shape
    factor = head_size ** (-0.5)
    key_count = key_rows.shape[1]
    key_block = math.gcd(key_count, 512)
    blocks = key_count // key_block

    def backward_advance(grad_query, element):
        part, grad_keys, grad_values = block_grads(
            queries,
            query_docs,
            grad_context,
            peak_log,
            delta,
            element[0],
            element[1],
            element[2],
            factor,
        )
        joined = None
        joined = jnp.concatenate(
            (
                grad_keys.reshape(seq_count, key_block, head_count * head_size),
                grad_values.reshape(seq_count, key_block, head_count * head_size),
            ),
            axis=2,
        )
        return (grad_query + part, joined)

    grad_query, joined = lax.scan(
        backward_advance,
        jnp.zeros(queries.shape, jnp.float32),
        (
            split_rows(key_rows, blocks, 1),
            split_rows(value_rows, blocks, 1),
            split_rows(key_docs, blocks, 1),
        ),
    )
    joined = jnp.moveaxis(joined, 0, 1).reshape(seq_count, key_count, 2 * head_count * head_size)
    return (grad_query, joined)


def on_device(
    tokens,
    segments,
    qkv_weight,
    qv_bias,
    attn_out_weight,
    attn_out_bias,
    norm1_gain,
    norm1_bias,
    up_weight,
    up_bias,
    down_weight,
    down_bias,
    norm2_gain,
    norm2_bias,
    cotangent,
):
    copies = jax.tree.map(
        lambda tensor: tensor.astype(jnp.bfloat16),
        (
            qkv_weight,
            qv_bias,
            attn_out_weight,
            attn_out_bias,
            norm1_gain,
            norm1_bias,
            up_weight,
            up_bias,
            down_weight,
            down_bias,
            norm2_gain,
            norm2_bias,
        ),
    )
    fetched = (
        lax.all_gather(copies[0], ("batch", "seq"), axis=1, tiled=True),
        lax.all_gather(copies[1], ("batch", "seq"), axis=1, tiled=True),
        lax.all_gather(copies[2], ("batch", "seq"), axis=0, tiled=True),
        lax.all_gather(copies[3], ("batch", "seq"), axis=0, tiled=True),
        lax.all_gather(copies[4], ("batch", "seq"), axis=0, tiled=True),
        lax.all_gather(copies[5], ("batch", "seq"), axis=0, tiled=True),
        lax.all_gather(copies[6], ("batch", "seq"), axis=0, tiled=True),
        lax.all_gather(copies[7], ("batch", "seq"), axis=0, tiled=True),
        lax.all_gather(copies[8], ("batch", "seq"), axis=0, tiled=True),
        lax.all_gather(copies[9], ("batch", "seq"), axis=0, tiled=True),
        lax.all_gather(copies[10], ("batch", "seq"), axis=0, tiled=True),
        lax.all_gather(copies[11], ("batch", "seq"), axis=0, tiled=True),
    )
    (
        triple,
        triple_bias,
        merger,
        merger_bias,
        gain_one,
        shift_one,
        widener,
        widen_bias,
        narrower,
        narrow_bias,
        gain_two,
        shift_two,
    ) = fetched
    rows_wide = tokens.astype(jnp.float32)
    seq_count, block_rows, width = tokens.shape
    head_count = width // HEAD_DIM
    offset = lax.axis_index("seq") * block_rows
    query_docs = lax.dynamic_slice_in_dim(segments, offset, block_rows, 1)
    projected = jnp.einsum("std,kde->kste", tokens, triple, preferred_element_type=jnp.float32)
    query_low = (projected[0] + triple_bias[0].astype(jnp.float32)).astype(jnp.bfloat16)
    key_low = projected[1].astype(jnp.bfloat16)
    value_low = (projected[2] + triple_bias[1].astype(jnp.float32)).astype(jnp.bfloat16)
    queries = query_low.reshape(seq_count, block_rows, head_count, HEAD_DIM)
    start_state = (
        jnp.full((seq_count, head_count, block_rows), masked_score, jnp.float32),
        jnp.zeros((seq_count, head_count, block_rows), jnp.float32),
        jnp.zeros((seq_count, head_count, block_rows, HEAD_DIM), jnp.float32),
    )
    pieces = (
        lax.all_gather(key_low, "seq", axis=1, tiled=True),
        lax.all_gather(value_low, "seq", axis=1, tiled=True),
    )
    count = pieces[0].shape[1]
    peak_new, row_sum, context = absorb_rows(
        start_state,
        queries,
        query_docs,
        pieces[0].reshape(seq_count, count, head_count, HEAD_DIM),
        pieces[1].reshape(seq_count, count, head_count, HEAD_DIM),
        segments,
    )
    context = context / row_sum[..., None]
    peak_log = peak_new + jnp.log(row_sum)
    context_heads = jnp.transpose(context, (0, 2, 1, 3))
    context_low = context_heads.reshape(seq_count, block_rows, width).astype(jnp.bfloat16)
    attn_branch = jnp.einsum(
        "ste,ed->std", context_low, merger, preferred_element_type=jnp.float32
    ) + merger_bias.astype(jnp.float32)
    mid_one = rows_wide + attn_branch
    hidden, norm_one_back = jax.vjp(
        layer_norm, mid_one, gain_one.astype(jnp.float32), shift_one.astype(jnp.float32)
    )
    hidden_low = hidden.astype(jnp.bfloat16)
    inner = jnp.einsum(
        "std,df->stf", hidden_low, widener, preferred_element_type=jnp.float32
    ) + widen_bias.astype(jnp.float32)
    act_low, gelu_back = jax.vjp(gelu_exact, inner)
    act_low = act_low.astype(jnp.bfloat16)
    ffn_branch = jnp.einsum(
        "stf,fd->std", act_low, narrower, preferred_element_type=jnp.float32
    ) + narrow_bias.astype(jnp.float32)
    final, norm_two_back = jax.vjp(
        layer_norm, hidden + ffn_branch, gain_two.astype(jnp.float32), shift_two.astype(jnp.float32)
    )
    output = final.astype(jnp.bfloat16)
    fetched = (
        lax.all_gather(copies[0], ("batch", "seq"), axis=1, tiled=True),
        lax.all_gather(copies[1], ("batch", "seq"), axis=1, tiled=True),
        lax.all_gather(copies[2], ("batch", "seq"), axis=0, tiled=True),
        lax.all_gather(copies[3], ("batch", "seq"), axis=0, tiled=True),
        lax.all_gather(copies[4], ("batch", "seq"), axis=0, tiled=True),
        lax.all_gather(copies[5], ("batch", "seq"), axis=0, tiled=True),
        lax.all_gather(copies[6], ("batch", "seq"), axis=0, tiled=True),
        lax.all_gather(copies[7], ("batch", "seq"), axis=0, tiled=True),
        lax.all_gather(copies[8], ("batch", "seq"), axis=0, tiled=True),
        lax.all_gather(copies[9], ("batch", "seq"), axis=0, tiled=True),
        lax.all_gather(copies[10], ("batch", "seq"), axis=0, tiled=True),
        lax.all_gather(copies[11], ("batch", "seq"), axis=0, tiled=True),
    )
    (
        triple,
        triple_bias,
        merger,
        merger_bias,
        gain_one,
        shift_one,
        widener,
        widen_bias,
        narrower,
        narrow_bias,
        gain_two,
        shift_two,
    ) = fetched
    grad_mid_two, grad_gain_two, grad_shift_two = norm_two_back(cotangent.astype(jnp.float32))
    grad_ffn = grad_mid_two.astype(jnp.bfloat16)
    grad_narrow_bias = jnp.sum(grad_ffn.astype(jnp.float32), axis=(0, 1))
    grad_narrower = jnp.einsum("stf,std->fd", act_low, grad_ffn, preferred_element_type=jnp.float32)
    grad_act = jnp.einsum("std,fd->stf", grad_ffn, narrower, preferred_element_type=jnp.float32)
    grad_inner = gelu_back(grad_act)[0].astype(jnp.bfloat16)
    grad_widen_bias = jnp.sum(grad_inner.astype(jnp.float32), axis=(0, 1))
    grad_widener = jnp.einsum(
        "std,stf->df", hidden_low, grad_inner, preferred_element_type=jnp.float32
    )
    grad_hidden = (
        jnp.einsum("stf,df->std", grad_inner, widener, preferred_element_type=jnp.float32)
        + grad_mid_two
    )
    grad_mid_one, grad_gain_one, grad_shift_one = norm_one_back(grad_hidden)
    grad_attn = grad_mid_one.astype(jnp.bfloat16)
    grad_merger_bias = jnp.sum(grad_attn.astype(jnp.float32), axis=(0, 1))
    grad_merger = jnp.einsum(
        "std,ste->de", context_low, grad_attn, preferred_element_type=jnp.float32
    )
    grad_context = jnp.einsum(
        "ste,de->std", grad_attn, merger, preferred_element_type=jnp.float32
    ).astype(jnp.bfloat16)
    grad_heads = grad_context.reshape(seq_count, block_rows, head_count, HEAD_DIM)
    delta = jnp.transpose(
        jnp.sum(grad_heads.astype(jnp.float32) * context_heads, axis=-1), (0, 2, 1)
    )
    key_flat, value_flat = (
        lax.all_gather(key_low, "seq", axis=1, tiled=True),
        lax.all_gather(value_low, "seq", axis=1, tiled=True),
    )
    key_all = key_flat.reshape(seq_count, -1, head_count, HEAD_DIM)
    value_all = value_flat.reshape(seq_count, -1, head_count, HEAD_DIM)
    grad_query, key_terms = backward_rows(
        queries, query_docs, grad_heads, peak_log, delta, key_all, value_all, segments
    )
    key_sums = lax.psum_scatter(
        key_terms.astype(jnp.bfloat16), "seq", scatter_dimension=1, tiled=True
    ).astype(jnp.float32)
    grad_key_low = key_sums[:, :, :width].astype(jnp.bfloat16)
    grad_value_low = key_sums[:, :, width:].astype(jnp.bfloat16)
    grad_query_low = grad_query.reshape(seq_count, block_rows, width).astype(jnp.bfloat16)
    stacked = jnp.stack((grad_query_low, grad_key_low, grad_value_low))
    grad_triple = jnp.einsum("std,kste->kde", tokens, stacked, preferred_element_type=jnp.float32)
    grad_triple_bias = jnp.stack(
        (
            jnp.sum(grad_query_low.astype(jnp.float32), axis=(0, 1)),
            jnp.sum(grad_value_low.astype(jnp.float32), axis=(0, 1)),
        )
    )
    grad_rows = (
        jnp.einsum("kste,kde->std", stacked, triple, preferred_element_type=jnp.float32)
        + grad_mid_one
    )
    owned = (
        lax.psum_scatter(grad_triple, ("batch", "seq"), scatter_dimension=1, tiled=True),
        lax.psum_scatter(grad_triple_bias, ("batch", "seq"), scatter_dimension=1, tiled=True),
        lax.psum_scatter(grad_merger, ("batch", "seq"), scatter_dimension=0, tiled=True),
        lax.psum_scatter(grad_merger_bias, ("batch", "seq"), scatter_dimension=0, tiled=True),
        lax.psum_scatter(grad_gain_one, ("batch", "seq"), scatter_dimension=0, tiled=True),
        lax.psum_scatter(grad_shift_one, ("batch", "seq"), scatter_dimension=0, tiled=True),
        lax.psum_scatter(grad_widener, ("batch", "seq"), scatter_dimension=0, tiled=True),
        lax.psum_scatter(grad_widen_bias, ("batch", "seq"), scatter_dimension=0, tiled=True),
        lax.psum_scatter(grad_narrower, ("batch", "seq"), scatter_dimension=0, tiled=True),
        lax.psum_scatter(grad_narrow_bias, ("batch", "seq"), scatter_dimension=0, tiled=True),
        lax.psum_scatter(grad_gain_two, ("batch", "seq"), scatter_dimension=0, tiled=True),
        lax.psum_scatter(grad_shift_two, ("batch", "seq"), scatter_dimension=0, tiled=True),
    )
    return (
        output,
        grad_rows.astype(jnp.bfloat16),
        owned[0],
        owned[1],
        owned[2],
        owned[3],
        owned[4],
        owned[5],
        owned[6],
        owned[7],
        owned[8],
        owned[9],
        owned[10],
        owned[11],
    )


def solution(mesh):
    return jax.shard_map(
        on_device,
        mesh=mesh,
        in_specs=(
            P("batch", "seq", None),
            P("batch", None),
            P(None, ("batch", "seq"), None),
            P(None, ("batch", "seq")),
            P(("batch", "seq"), None),
            P(("batch", "seq")),
            P(("batch", "seq")),
            P(("batch", "seq")),
            P(("batch", "seq"), None),
            P(("batch", "seq")),
            P(("batch", "seq"), None),
            P(("batch", "seq")),
            P(("batch", "seq")),
            P(("batch", "seq")),
            P("batch", "seq", None),
        ),
        out_specs=(
            P("batch", "seq", None),
            P("batch", "seq", None),
            P(None, ("batch", "seq"), None),
            P(None, ("batch", "seq")),
            P(("batch", "seq"), None),
            P(("batch", "seq")),
            P(("batch", "seq")),
            P(("batch", "seq")),
            P(("batch", "seq"), None),
            P(("batch", "seq")),
            P(("batch", "seq"), None),
            P(("batch", "seq")),
            P(("batch", "seq")),
            P(("batch", "seq")),
        ),
        check_vma=False,
    )
```

profile of v0, /device:TPU:0, one launch (start us, length us, event | category | flops | bytes accessed | tf_op | source)
XLA Modules:
  0.0 1189.3 jit_solution(99178124049490004)
XLA Ops:
  9.6 69.8 %all-gather.1 = bf16[32,24,2]{1,2,0:T(2,128)(2,1)S(1)} all-gather(bf16[1,24,2]{1,2,0:T(2,128)(2,1)S(1)} %convert_bitcast_fusion), channel_id=1, replica_groups=mesh['batch'=8,'seq'=4] {'batch','seq'}, dimensions={0}, use_global_device_ids=true | all-gather | bytes 3168 | tf_op jit(solution)/shard_map/all_gather | solution.py:191
  79.5 4.3 convolution_bitcast_fusion.1
  93.6 38.1 %all-reduce.17 = (bf16[768]{0:T(1024)(128)(2,1)S(1)}, bf16[768]{0:T(1024)(128)(2,1)S(1)}, bf16[768]{0:T(1024)(128)(2,1)S(1)}, bf16[3072]{0:T(1024)(128)(2,1)S(1)...) all-reduce(bf16[768]{0:T(1024)(128)(2,1)S(1)} %dynamic-update-slice, ...), channel_id=1, replica_groups=mesh['batch'=8,'seq'=4] {'batch','seq'}, use_global_device_ids=true, to_apply=%add | all-reduce | flops 7680 | bytes 30720
  133.6 6.3 transpose_reshape_reshape.9
  144.2 29.7 %all-gather.19.cloned.1.call-done = bf16[1,1,2048,768]{2,3,0,1:T(8,128)(2,1)} async-done(((bf16[1,1,512,768]{2,3,0,1:T(8,128)(2,1)}), bf16[1,1,2048,768]{2,3,0,1:T(8,128)(2,1)}) %all-gather.19.cloned.1.call-update) | async-done | bytes 3145744 | tf_op jit(solution)/shard_map/all_gather | solution.py:233
  173.9 6.2 transpose_reshape_reshape.8
  180.0 4.3 copy.64
  184.4 78.6 %while.28 = (s32[]{:T(128)}, f32[1,12,512]{2,1,0:T(8,128)S(1)}, f32[1,12,512]{2,1,0:T(8,128)S(1)}, f32[1,12,512,64]{2,3,1,0:T(8,128)S(1)}, s32[1,512]{1,0:T(1,12...) while((s32[]{:T(128)}, f32[1,12,512]{2,1,0:T(8,128)S(1)}, ...), condition=%wide.region_3.4_spmd.clone, body=%wide.region_0.3_spmd.clone.sunk | while | flops 847679488 | bytes 95036568 | solution.py:70
  184.6 7.7 fusion.125
  192.3 6.7 bitcast_add_fusion.11
  204.2 7.7 fusion.125
  211.9 6.7 bitcast_add_fusion.11
  223.9 7.7 fusion.125
  231.6 6.7 bitcast_add_fusion.11
  243.5 7.7 fusion.125
  251.2 6.7 bitcast_add_fusion.11
  267.4 29.7 %all-gather.15.cloned.1.call-done = bf16[768,3072]{1,0:T(8,128)(2,1)} async-done(((bf16[24,3072]{1,0:T(8,128)(2,1)}), bf16[768,3072]{1,0:T(8,128)(2,1)}) %all-gather.15.cloned.1.call-update) | async-done | bytes 4718608 | tf_op jit(solution)/shard_map/all_gather | solution.py:196
  297.0 21.0 %multiply_convert_fusion = (bf16[512,3072]{1,0:T(8,128)(2,1)}, f32[512,3072]{1,0:T(8,128)}, f32[512,3072]{1,0:T(8,128)}) fusion(f32[3072]{0:T(1024)S(1)} %convert_element_type.254, bf16[768,3072]{1,0:T(8,128)(2,1)} %all-gather.15.cloned.1.call-done, f32[1,512,768]{2,1,0:T(8,128)} %copy-done.7, f32[768]{0:T(1024)S(1)} %convert_element_type.250, ...), kind=kOutput, calls=%fused_computation.63 | convolution fusion | flops 2521694208 | bytes 22042624 | tf_op jit(solution)/shard_map/std,df->stf/dot_general | solution.py:257
  318.0 44.3 %all-gather.17.cloned.1.call-done = bf16[3072,768]{1,0:T(8,128)(2,1)} async-done(((bf16[96,768]{1,0:T(8,128)(2,1)}), bf16[3072,768]{1,0:T(8,128)(2,1)}) %all-gather.17.cloned.1.call-update) | async-done | bytes 4718608 | tf_op jit(solution)/shard_map/all_gather | solution.py:198
  362.3 6.5 fusion.87
  373.0 9.0 convert_reduce_fusion
  392.7 112.6 %while.29 = (s32[]{:T(128)}, f32[1,512,12,64]{1,3,2,0:T(8,128)}, bf16[4,1,512,1536]{2,3,1,0:T(8,128)(2,1)}, bf16[4,1,512,12,64]{2,4,3,1,0:T(8,128)(2,1)}, s32[1,...) while((s32[]{:T(128)}, f32[1,512,12,64]{1,3,2,0:T(8,128)}, ...), condition=%wide.region_14.15_spmd.clone, body=%wide.region_13.14_spmd.clone.sunk | while | flops 2056388608 | bytes 121194840 | solution.py:142
  397.3 5.6 fusion.139
  403.0 4.6 convolution_multiply_fusion.2
  407.6 5.1 fusion.140
  425.5 5.6 fusion.139
  431.1 4.6 convolution_multiply_fusion.2
  435.7 5.1 fusion.140
  443.6 4.3 bitcast_add_fusion.12
  453.6 5.6 fusion.139
  459.3 4.6 convolution_multiply_fusion.2
  463.9 5.1 fusion.140
  481.7 5.6 fusion.139
  487.4 4.6 convolution_multiply_fusion.2
  492.0 5.1 fusion.140
  499.9 4.3 bitcast_add_fusion.12
  505.3 8.7 copy.69
  515.9 66.6 %reduce-scatter.6.cloned.1.call-done = bf16[1,512,1536]{2,1,0:T(8,128)(2,1)} async-done(((bf16[1,2048,1536]{2,1,0:T(8,128)(2,1)}), bf16[1,512,1536]{2,1,0:T(8,128)(2,1)}) %reduce-scatter.6.cloned.1.call-update) | async-done | bytes 1572880 | tf_op jit(solution)/shard_map/reduce_scatter | solution.py:333
  585.1 4.9 convolution_bitcast_fusion
  590.1 11.0 copy.73
  604.8 7.3 fusion.79
  613.3 8.4 fusion.65
  623.3 41.2 %all-reduce.16 = (f32[2,768]{1,0:T(2,128)S(1)}, f32[768]{0:T(1024)S(1)}, f32[768]{0:T(1024)S(1)}, f32[768]{0:T(1024)S(1)}, f32[3072]{0:T(1024)S(1)}, /*index=5*/...) all-reduce(f32[2,768]{1,0:T(2,128)S(1)} %pad_maximum_fusion, ...), channel_id=5, replica_groups=mesh['batch'=8,'seq'=4] {'batch','seq'}, use_global_device_ids=true, to_apply=%region_19.20.clone | all-reduce | flops 9216 | bytes 73728
  669.3 5.7 fusion.58
  675.0 118.6 %all-reduce.20.cloned.1.call-done = f32[3,768,768]{2,0,1:T(4,128)} async-done(((f32[3,768,768]{2,0,1:T(4,128)}), f32[3,768,768]{2,0,1:T(4,128)}) %all-reduce.20.cloned.1.call-update) | async-done | bytes 7077904
  795.4 103.8 %reduce-scatter.8.cloned.1.call-done = f32[24,768]{1,0:T(8,128)} async-done(((f32[768,768]{1,0:T(8,128)}), f32[24,768]{1,0:T(8,128)}) %reduce-scatter.8.cloned.1.call-update) | async-done | bytes 73744 | tf_op jit(solution)/shard_map/reduce_scatter | solution.py:354
  899.2 141.5 %reduce-scatter.10.cloned.1.call-done = f32[24,3072]{1,0:T(8,128)} async-done(((f32[768,3072]{1,0:T(8,128)}), f32[24,3072]{1,0:T(8,128)}) %reduce-scatter.10.cloned.1.call-update) | async-done | bytes 294928 | tf_op jit(solution)/shard_map/reduce_scatter | solution.py:358
  1040.7 141.6 %reduce-scatter.12.cloned.1.call-done = f32[96,768]{1,0:T(8,128)} async-done(((f32[3072,768]{1,0:T(8,128)}), f32[96,768]{1,0:T(8,128)}) %reduce-scatter.12.cloned.1.call-update) | async-done | bytes 294928 | tf_op jit(solution)/shard_map/reduce_scatter | solution.py:360
  (324 shorter events, 117.5 us)
Async XLA Ops:
  7.2 72.3 %all-gather.9.cloned.1.call-start = ((), (), s32[]{:S(2)}) async-start(), calls=%async_computation.4 | async-start | bytes 3649536 | tf_op jit(solution)/shard_map/all_gather | solution.py:190
  8.8 124.7 %all-gather.11.cloned.1.call-start = ((), (), s32[]{:S(2)}) async-start(), calls=%async_computation.5 | async-start | bytes 3932160 | tf_op jit(solution)/shard_map/all_gather | solution.py:234
  83.9 5.8 copy-start.28
  83.9 6.5 copy-start.26
  83.9 7.2 copy-start.27
  86.0 6.0 copy-start.50
  86.0 6.0 copy-start.51
  86.0 6.0 copy-start.52
  86.0 6.0 copy-start.53
  86.0 6.1 copy-start.54
  86.0 6.1 copy-start.55
  86.0 6.1 copy-start.56
  86.0 45.8 %copy-start.29 = (s32[1,2048]{1,0:T(1,128)S(1)}, s32[1,2048]{1,0:T(1,128)}, u32[]{:S(2)}) copy-start(s32[1,2048]{1,0:T(1,128)} %param.20) | copy-start | bytes 24580
  87.1 86.7 %all-gather.19.cloned.1.call-start = ((), (), s32[]{:S(2)}) async-start(), calls=%async_computation.13 | async-start | bytes 3932160 | tf_op jit(solution)/shard_map/all_gather | solution.py:233
  89.6 173.6 %all-gather.13.cloned.1.call-start = ((), (), s32[]{:S(2)}) async-start(), calls=%async_computation.6 | async-start | bytes 1216512 | tf_op jit(solution)/shard_map/all_gather | solution.py:192
  90.3 206.7 %all-gather.15.cloned.1.call-start = ((), (), s32[]{:S(2)}) async-start(), calls=%async_computation.7 | async-start | bytes 4866048 | tf_op jit(solution)/shard_map/all_gather | solution.py:196
  91.1 271.2 %all-gather.17.cloned.1.call-start = ((), (), s32[]{:S(2)}) async-start(), calls=%async_computation.8 | async-start | bytes 4866048 | tf_op jit(solution)/shard_map/all_gather | solution.py:198
  91.8 490.6 %reduce-scatter.6.cloned.1.call-start = ((), (), s32[]{:S(2)}) async-start(), calls=%async_computation.9 | async-start | bytes 7864320 | tf_op jit(solution)/shard_map/reduce_scatter | solution.py:333
  131.8 254.0 %copy-start.36 = (f32[768]{0:T(1024)}, f32[768]{0:T(1024)S(1)}, u32[]{:S(2)}) copy-start(f32[768]{0:T(1024)S(1)} %convert_element_type.248) | copy-start | bytes 9220
  131.8 230.5 %copy-start.43 = (f32[768]{0:T(1024)}, f32[768]{0:T(1024)S(1)}, u32[]{:S(2)}) copy-start(f32[768]{0:T(1024)S(1)} %convert_element_type.250) | copy-start | bytes 9220
  192.3 8.4 copy-start
  211.9 8.6 copy-start
  231.6 8.4 copy-start
  251.2 8.5 copy-start
  265.9 119.8 %copy-start.30 = (f32[512]{0:T(512)}, f32[512]{0:T(512)S(1)}, u32[]{:S(2)}) copy-start(f32[512]{0:T(512)S(1)} %broadcast_multiply_fusion.1) | copy-start | bytes 6148
  267.4 118.4 %copy-start.39 = (f32[512]{0:T(512)}, f32[512]{0:T(512)S(1)}, u32[]{:S(2)}) copy-start(f32[512]{0:T(512)S(1)} %fusion.75) | copy-start | bytes 6148
  362.3 6.9 copy-start.14
  372.0 10.0 slice-start
  372.8 9.2 copy-start.22
  373.0 9.0 copy-start.8
  373.0 9.0 slice-start.1
  386.4 5.9 copy-start.41
  415.4 5.5 copy-start.3
  415.4 5.5 copy-start.16
  443.6 5.5 copy-start.3
  443.6 5.5 copy-start.16
  471.7 5.4 copy-start.3
  471.7 5.5 copy-start.16
  499.9 5.5 copy-start.3
  499.9 5.5 copy-start.16
  514.0 279.6 %all-reduce.20.cloned.1.call-start = ((), (), s32[]{:S(2)}) async-start(), calls=%async_computation.14 | async-start | bytes 18874368
  515.4 69.8 %copy-start.49 = (bf16[1,512,768]{2,1,0:T(8,128)(2,1)S(1)}, bf16[1,512,768]{2,1,0:T(8,128)(2,1)}, u32[]{:S(2)}) copy-start(bf16[1,512,768]{2,1,0:T(8,128)(2,1)} %param.19) | copy-start | bytes 2359300
  515.9 74.2 %copy-start.21 = (bf16[1,1,512,768]{3,2,0,1:T(8,128)(2,1)}, bf16[1,1,512,768]{3,2,0,1:T(8,128)(2,1)S(1)}, u32[]{:S(2)}) copy-start(bf16[1,1,512,768]{3,2,0,1:T(8,128)(2,1)S(1)} %copy.70) | copy-start | bytes 2359300
  601.1 298.1 %reduce-scatter.8.cloned.1.call-start = ((), (), s32[]{:S(2)}) async-start(), calls=%async_computation.10 | async-start | bytes 2433024 | tf_op jit(solution)/shard_map/reduce_scatter | solution.py:354
  604.7 436.0 %reduce-scatter.10.cloned.1.call-start = ((), (), s32[]{:S(2)}) async-start(), calls=%async_computation.11 | async-start | bytes 9732096 | tf_op jit(solution)/shard_map/reduce_scatter | solution.py:358
  612.2 570.2 %reduce-scatter.12.cloned.1.call-start = ((), (), s32[]{:S(2)}) async-start(), calls=%async_computation.12 | async-start | bytes 9732096 | tf_op jit(solution)/shard_map/reduce_scatter | solution.py:360
  621.7 47.6 %copy-start.11 = (f32[1,512,768]{2,1,0:T(8,128)S(1)}, f32[1,512,768]{2,1,0:T(8,128)}, u32[]{:S(2)}) copy-start(f32[1,512,768]{2,1,0:T(8,128)} %copy-done.10) | copy-start | bytes 4718596
  621.7 47.6 %copy-start.42 = (f32[512]{0:T(512)S(1)}, f32[512]{0:T(512)}, u32[]{:S(2)}) copy-start(f32[512]{0:T(512)} %copy-done.41) | copy-start | bytes 6148
  (47 other events, 99.6 us)
Sparse Core Ops, SparseCore 0:
  11.4 62.7 all-gather.8
  87.3 40.2 all-gather.10
  130.0 43.8 all-gather.18
  177.2 53.9 all-gather.12
  234.5 62.4 all-gather.14
  300.4 61.8 all-gather.16
  514.1 68.3 reduce-scatter.5
  601.2 192.3 all-reduce.19
  799.5 99.6 reduce-scatter.7
  905.5 135.1 reduce-scatter.9
  1047.2 135.0 reduce-scatter.11
where the time goes:
time: 1200 us; the launch traced here: 1190 us
  waiting for transfers between devices  676 us (56%)
  matrix products  226 us (19%)
  blocking collectives  149 us (12%)
  local copies, waits for them, and re-layouts  83.6 us (7%)
  other arithmetic  37.7 us (3%)
  between operations  15.1 us (1%)
    reduce_scatter x1, waiting for transfers between devices, on_device(): lax.psum_scatter(grad_narrower, ('batch', 'seq'), scatter_dimension=0, ti...  142 us
    reduce_scatter x1, waiting for transfers between devices, on_device(): lax.psum_scatter(grad_widener, ('batch', 'seq'), scatter_dimension=0, til...  142 us
    unnamed x12, waiting for transfers between devices  119 us
    reduce_scatter x1, waiting for transfers between devices, on_device(): lax.psum_scatter(grad_merger, ('batch', 'seq'), scatter_dimension=0, tile...  104 us
    unnamed x2, blocking collectives  79.4 us
    all_gather x1, blocking collectives, on_device(): lax.all_gather(copies[1], ('batch', 'seq'), axis=1, tiled=True)  69.8 us
    reduce_scatter x1, waiting for transfers between devices, on_device(): lax.psum_scatter(key_terms.astype(jnp.bfloat16), 'seq', scatter_dimension...  66.6 us
    all_gather x1, waiting for transfers between devices, on_device(): lax.all_gather(copies[8], ('batch', 'seq'), axis=0, tiled=True)  44.3 us
  transfers between devices with their start and end apart: 11, of which 8 were waited for; matrix products, arithmetic and copies ran while one was open for 13% of the time, Pallas kernels for 0%

commit v1 on v0

v1 whole, which is shorter than its diff:
```python
import functools
import math

import jax
import jax.numpy as jnp
from jax import lax
from jax.experimental import pallas as pl
from jax.experimental.pallas import tpu as pltpu
from jax.sharding import PartitionSpec as P

HEAD_DIM = 64
epsilon = 1e-05
masked_score = -1e30
F32 = jnp.float32
BF16 = jnp.bfloat16
ANY = pl.BlockSpec(memory_space=pl.ANY)
INV = pl.BlockSpec(memory_space=pltpu.VMEM)
INS = pl.BlockSpec(memory_space=pltpu.SMEM)


def dot_nn(a, b):
    return lax.dot_general(a, b, (((1,), (0,)), ((), ())), preferred_element_type=F32)


def dot_nt(a, b):
    return lax.dot_general(a, b, (((1,), (1,)), ((), ())), preferred_element_type=F32)


def dot_tn(a, b):
    return lax.dot_general(a, b, (((0,), (0,)), ((), ())), preferred_element_type=F32)


def turn_docs(doc_row_ref, doc_turned, span, block):
    doc_turned[span, :] = jnp.broadcast_to(doc_row_ref[:, span], (128, block)).T


def doc_column(doc_turned, span, block):
    docs = doc_turned[span, :]
    return jnp.concatenate([docs] * (block // 128), axis=1)


def attend_kernel(
    heads, block, low_ref, high_ref, rows_ref, weight_ref, bias_ref, doc_row_ref,
    query_ref, key_ref, value_ref, context_ref, turned_ref, log_ref,
    value_turned, doc_turned, scores,
):
    length, width = rows_ref.shape
    wide = heads * HEAD_DIM
    count = length // block

    def project(i, carry):
        span = pl.ds(pl.multiple_of(i * block, block), block)
        rows = rows_ref[span, :]
        turn_docs(doc_row_ref, doc_turned, span, block)
        for part in range(3):
            made = dot_nn(rows, weight_ref[part]) + bias_ref[part][None, :]
            made = made.astype(BF16)
            if part == 0:
                made = made * jnp.asarray(HEAD_DIM ** (-0.5), BF16)
            if part == 2:
                value_turned[:, span] = made.T
            target = (query_ref, key_ref, value_ref)[part]
            for h in range(heads):
                target[h, span, :] = made[:, h * HEAD_DIM : (h + 1) * HEAD_DIM]
        return carry

    lax.fori_loop(0, count, project, 0)

    def one_block(i, carry):
        span = pl.ds(pl.multiple_of(i * block, block), block)
        query_docs = doc_row_ref[:, span]
        queries = [query_ref[h, span, :] for h in range(heads)]

        def score(j, peaks):
            keys_at = pl.ds(pl.multiple_of(j * block, block), block)
            same = doc_column(doc_turned, keys_at, block) == query_docs
            out = []
            for h in range(heads):
                value = jnp.where(same, dot_nt(key_ref[h, keys_at, :], queries[h]), masked_score)
                scores[h, keys_at, :] = value
                out.append(jnp.maximum(peaks[h], jnp.max(value.reshape(-1, 8, block), axis=0)))
            return tuple(out)

        first = (jnp.full((8, block), masked_score, F32),) * heads
        peaks = lax.fori_loop(low_ref[i], high_ref[i], score, first)
        peaks = [jnp.max(peak, axis=0, keepdims=True) for peak in peaks]

        def absorb(j, state):
            keys_at = pl.ds(pl.multiple_of(j * block, block), block)
            out = []
            for h in range(heads):
                total, context = state[2 * h : 2 * h + 2]
                weights = jnp.exp(scores[h, keys_at, :] - peaks[h])
                total = total + jnp.sum(weights.reshape(-1, 8, block), axis=0)
                context = context + dot_nn(
                    value_turned[h * HEAD_DIM : (h + 1) * HEAD_DIM, keys_at], weights.astype(BF16)
                )
                out += [total, context]
            return tuple(out)

        start = (jnp.zeros((8, block), F32), jnp.zeros((HEAD_DIM, block), F32)) * heads
        state = lax.fori_loop(low_ref[i], high_ref[i], absorb, start)
        for h in range(heads):
            total = jnp.sum(state[2 * h], axis=0, keepdims=True)
            turned_ref[h * HEAD_DIM : (h + 1) * HEAD_DIM, span] = state[2 * h + 1] / total
            log_ref[h : h + 1, span] = peaks[h] + jnp.log(total)
        context_ref[span, :] = turned_ref[:, span].T.astype(BF16)
        return carry

    lax.fori_loop(0, count, one_block, 0)


def attend(rows, weight, bias, docs, low, high, block):
    length, width = rows.shape
    wide = weight.shape[2]
    heads = wide // HEAD_DIM
    shape = jax.ShapeDtypeStruct
    return pl.pallas_call(
        functools.partial(attend_kernel, heads, block),
        out_shape=(
            shape((heads, length, HEAD_DIM), BF16),
            shape((heads, length, HEAD_DIM), BF16),
            shape((heads, length, HEAD_DIM), BF16),
            shape((length, wide), BF16),
            shape((wide, length), F32),
            shape((heads, length), F32),
        ),
        in_specs=[INS, INS, INV, INV, INV, INV],
        out_specs=(INV,) * 6,
        scratch_shapes=[
            pltpu.VMEM((wide, length), BF16),
            pltpu.VMEM((length, 128), jnp.int32),
            pltpu.VMEM((heads, length, block), F32),
        ],
        compiler_params=pltpu.CompilerParams(vmem_limit_bytes=60 << 20),
        name="attend",
    )(low, high, rows, weight, bias, docs.reshape(1, length))


def attend_back_kernel(
    heads, block, low_ref, high_ref, rows_ref, weight_ref, doc_row_ref,
    query_ref, key_ref, value_ref, turned_ref, log_ref, grad_ref,
    part_ref, weight_grad_ref, bias_grad_ref,
    query_turned, key_turned, grad_heads, delta, joined, doc_turned,
):
    length, width = rows_ref.shape
    wide = heads * HEAD_DIM
    count = length // block

    def prepare(i, carry):
        span = pl.ds(pl.multiple_of(i * block, block), block)
        turn_docs(doc_row_ref, doc_turned, span, block)
        grad = grad_ref[span, :]
        turned = grad.astype(F32).T
        product = turned * turned_ref[:, span]
        for h in range(heads):
            part = slice(h * HEAD_DIM, (h + 1) * HEAD_DIM)
            delta[h : h + 1, span] = jnp.sum(product[part, :], axis=0, keepdims=True)
            grad_heads[h, span, :] = grad[:, part]
            key_turned[part, span] = key_ref[h, span, :].T
        query_turned[:, span] = jnp.zeros((wide, block), F32)
        return carry

    lax.fori_loop(0, count, prepare, 0)

    def one_block(j, carry):
        keys_at = pl.ds(pl.multiple_of(j * block, block), block)
        key_docs = doc_column(doc_turned, keys_at, block)
        keys = [key_ref[h, keys_at, :] for h in range(heads)]
        values = [value_ref[h, keys_at, :] for h in range(heads)]

        def absorb(i, state):
            span = pl.ds(pl.multiple_of(i * block, block), block)
            same = key_docs == doc_row_ref[:, span]
            out = []
            for h in range(heads):
                part = slice(h * HEAD_DIM, (h + 1) * HEAD_DIM)
                grad_key, grad_value = state[2 * h : 2 * h + 2]
                queries = query_ref[h, span, :]
                grads = grad_heads[h, span, :]
                scores = dot_nt(keys[h], queries)
                probs = jnp.where(same, jnp.exp(scores - log_ref[h : h + 1, span]), 0.0)
                grad_probs = dot_nt(values[h], grads)
                grad_scores = (probs * (grad_probs - delta[h : h + 1, span])).astype(BF16)
                grad_value = grad_value + dot_nn(probs.astype(BF16), grads)
                grad_key = grad_key + dot_nn(grad_scores, queries)
                query_turned[part, span] += dot_nn(key_turned[part, keys_at], grad_scores)
                out += [grad_key, grad_value]
            return tuple(out)

        start = (jnp.zeros((block, HEAD_DIM), F32),) * (2 * heads)
        state = lax.fori_loop(low_ref[j], high_ref[j], absorb, start)
        grad_key = jnp.concatenate(state[0::2], axis=1)
        grad_value = jnp.concatenate(state[1::2], axis=1)
        joined[1, keys_at, :] = grad_key.astype(BF16)
        joined[2, keys_at, :] = grad_value.astype(BF16)
        return carry

    lax.fori_loop(0, count, one_block, 0)

    def finish(i, sums):
        span = pl.ds(pl.multiple_of(i * block, block), block)
        grad_query = (query_turned[:, span].T * (HEAD_DIM ** (-0.5))).astype(BF16)
        joined[0, span, :] = grad_query
        rows = dot_nt(grad_query, weight_ref[0])
        rows = rows + dot_nt(joined[1, span, :], weight_ref[1])
        rows = rows + dot_nt(joined[2, span, :], weight_ref[2])
        part_ref[span, :] = rows.astype(BF16)
        return (
            sums[0] + jnp.sum(grad_query.astype(F32), axis=0, keepdims=True),
            sums[1] + jnp.sum(joined[2, span, :].astype(F32), axis=0, keepdims=True),
        )

    zero = jnp.zeros((1, wide), F32)
    sums = lax.fori_loop(0, count, finish, (zero, zero))
    bias_grad_ref[0:1, :] = sums[0]
    bias_grad_ref[1:2, :] = sums[1]
    tile = 256

    def weight_rows(i, carry):
        at = pl.ds(pl.multiple_of(i * tile, tile), tile)
        turned = rows_ref[:, at].T
        for part in range(3):
            weight_grad_ref[part, at, :] = dot_nn(turned, joined[part]).astype(BF16)
        return carry

    lax.fori_loop(0, width // tile, weight_rows, 0)


def attend_back(rows, weight, docs, low, high, query, key, value, turned, log, grad, block):
    length, width = rows.shape
    wide = weight.shape[2]
    heads = wide // HEAD_DIM
    shape = jax.ShapeDtypeStruct
    return pl.pallas_call(
        functools.partial(attend_back_kernel, heads, block),
        out_shape=(
            shape((length, width), BF16),
            shape((3, width, wide), BF16),
            shape((2, wide), F32),
        ),
        in_specs=[INS, INS] + [INV] * 9,
        out_specs=(INV,) * 3,
        scratch_shapes=[
            pltpu.VMEM((wide, length), F32),
            pltpu.VMEM((wide, length), BF16),
            pltpu.VMEM((heads, length, HEAD_DIM), BF16),
            pltpu.VMEM((heads, length), F32),
            pltpu.VMEM((3, length, wide), BF16),
            pltpu.VMEM((length, 128), jnp.int32),
        ],
        compiler_params=pltpu.CompilerParams(vmem_limit_bytes=60 << 20),
        name="attend_back",
    )(
        low, high, rows, weight, docs.reshape(1, length),
        query, key, value, turned, log, grad,
    )


def normalize(values):
    centre = jnp.mean(values, axis=-1, keepdims=True)
    centred = values - centre
    spread = jnp.mean(centred * centred, axis=-1, keepdims=True)
    scale = lax.rsqrt(spread + epsilon)
    return centred * scale, scale


def normalize_back(grad, normal, scale):
    first = jnp.mean(grad, axis=-1, keepdims=True)
    second = jnp.mean(grad * normal, axis=-1, keepdims=True)
    return scale * (grad - first - normal * second)


def add_rows(values):
    return jnp.sum(values, axis=0, keepdims=True)


def dense_kernel(
    step, chunk, context_ref, tokens_ref, cotangent_ref, vector_ref, wide_ref,
    merger_hbm, widener_hbm, narrower_hbm,
    output_ref, grad_context_ref, grad_mid_ref, grad_merger_ref, grad_widener_ref,
    grad_narrower_ref, sums_ref, wide_sum_ref,
    merger, widener, narrower, hidden, hidden_low, normal_one, scale_one, act, slope, branch,
    mid_two, grad_ffn, sems,
):
    rows, width = tokens_ref.shape
    inner = widener.shape[1]
    pieces = inner // chunk
    steps = rows // step
    copies = [
        pltpu.make_async_copy(merger_hbm, merger, sems.at[0]),
        pltpu.make_async_copy(widener_hbm, widener, sems.at[1]),
        pltpu.make_async_copy(narrower_hbm, narrower, sems.at[2]),
    ]
    for copy in copies:
        copy.start()
    merger_bias, gain_one, shift_one, narrow_bias, gain_two, shift_two = (
        vector_ref[i : i + 1, :] for i in range(6)
    )
    sums_ref[...] = jnp.zeros_like(sums_ref)
    wide_sum_ref[...] = jnp.zeros_like(wide_sum_ref)
    copies[0].wait()
    for i in range(steps):
        span = slice(i * step, (i + 1) * step)
        mid = tokens_ref[span, :].astype(F32) + (
            dot_nn(context_ref[span, :], merger[...]) + merger_bias
        )
        normal, scale = normalize(mid)
        normal_one[span, :] = normal
        scale_one[span, :] = scale
        value = normal * gain_one + shift_one
        hidden[span, :] = value
        hidden_low[span, :] = value.astype(BF16)
    copies[1].wait()
    copies[2].wait()
    branch[...] = jnp.zeros_like(branch)

    def widen(j, carry):
        at = pl.ds(pl.multiple_of(j * chunk, chunk), chunk)
        bias = wide_ref[:, at]
        for i in range(steps):
            span = slice(i * step, (i + 1) * step)
            value = dot_nn(hidden_low[span, :], widener[:, at]) + bias
            half = 0.5 + 0.5 * lax.erf(value * (2.0 ** -0.5))
            low = (value * half).astype(BF16)
            act[span, at] = low
            slope[span, at] = (
                half + value * (jnp.exp(-0.5 * value * value) * (1.0 / math.sqrt(2.0 * math.pi)))
            ).astype(slope.dtype)
            branch[span, :] += dot_nn(low, narrower[at, :])
        return carry

    lax.fori_loop(0, pieces, widen, 0)
    for i in range(steps):
        span = slice(i * step, (i + 1) * step)
        normal, scale = normalize(hidden[span, :] + (branch[span, :] + narrow_bias))
        output_ref[span, :] = (normal * gain_two + shift_two).astype(BF16)
        grad = cotangent_ref[span, :].astype(F32)
        grad_mid = normalize_back(grad * gain_two, normal, scale)
        mid_two[span, :] = grad_mid
        low = grad_mid.astype(BF16)
        grad_ffn[span, :] = low
        sums_ref[3:4, :] += add_rows(low.astype(F32))
        sums_ref[4:5, :] += add_rows(grad * normal)
        sums_ref[5:6, :] += add_rows(grad)

    def narrow_back(j, carry):
        at = pl.ds(pl.multiple_of(j * chunk, chunk), chunk)
        grad_narrower_ref[at, :] = dot_tn(act[:, at], grad_ffn[...]).astype(grad_narrower_ref.dtype)
        total = jnp.zeros((1, chunk), F32)
        for i in range(steps):
            span = slice(i * step, (i + 1) * step)
            value = dot_nt(grad_ffn[span, :], narrower[at, :]) * slope[span, at].astype(F32)
            low = value.astype(BF16)
            total = total + add_rows(low.astype(F32))
            act[span, at] = low
            mid_two[span, :] += dot_nt(low, widener[:, at])
        wide_sum_ref[:, at] = total
        grad_widener_ref[:, at] = dot_tn(hidden_low[...], act[:, at]).astype(grad_widener_ref.dtype)
        return carry

    lax.fori_loop(0, pieces, narrow_back, 0)
    for i in range(steps):
        span = slice(i * step, (i + 1) * step)
        grad = mid_two[span, :]
        normal = normal_one[span, :]
        grad_mid = normalize_back(grad * gain_one, normal, scale_one[span, :])
        grad_mid_ref[span, :] = grad_mid
        low = grad_mid.astype(BF16)
        grad_ffn[span, :] = low
        sums_ref[0:1, :] += add_rows(low.astype(F32))
        sums_ref[1:2, :] += add_rows(grad * normal)
        sums_ref[2:3, :] += add_rows(grad)
        grad_context_ref[span, :] = dot_nt(low, merger[...]).astype(BF16)
    grad_merger_ref[...] = dot_tn(context_ref[...], grad_ffn[...]).astype(grad_merger_ref.dtype)


def dense(context, tokens, cotangent, vectors, wide_bias, merger, widener, narrower):
    rows, width = tokens.shape
    inner = widener.shape[1]
    shape = jax.ShapeDtypeStruct
    return pl.pallas_call(
        functools.partial(dense_kernel, 256, 512),
        out_shape=(
            shape((rows, width), BF16),
            shape((rows, width), BF16),
            shape((rows, width), F32),
            shape((width, width), BF16),
            shape((width, inner), BF16),
            shape((inner, width), BF16),
            shape((8, width), F32),
            shape((1, inner), F32),
        ),
        in_specs=[INV] * 5 + [ANY] * 3,
        out_specs=(INV,) * 8,
        scratch_shapes=[
            pltpu.VMEM((width, width), BF16),
            pltpu.VMEM((width, inner), BF16),
            pltpu.VMEM((inner, width), BF16),
            pltpu.VMEM((rows, width), F32),
            pltpu.VMEM((rows, width), BF16),
            pltpu.VMEM((rows, width), F32),
            pltpu.VMEM((rows, 1), F32),
            pltpu.VMEM((rows, inner), BF16),
            pltpu.VMEM((rows, inner), BF16),
            pltpu.VMEM((rows, width), F32),
            pltpu.VMEM((rows, width), F32),
            pltpu.VMEM((rows, width), BF16),
            pltpu.SemaphoreType.DMA((3,)),
        ],
        compiler_params=pltpu.CompilerParams(vmem_limit_bytes=63 << 20),
        name="dense",
    )(context, tokens, cotangent, vectors, wide_bias, merger, widener, narrower)


def block_ranges(docs, block):
    grouped = docs.reshape(-1, block)
    low = jnp.sum((docs[None, :] < grouped[:, :1]).astype(jnp.int32), axis=1) // block
    high = jnp.sum((docs[None, :] <= grouped[:, -1:]).astype(jnp.int32), axis=1)
    return low, (high + block - 1) // block


def spread(parts):
    return jnp.transpose(parts, (1, 0, 2)).reshape(parts.shape[1], -1)


class PlainLinks:
    def __init__(self, mesh, seqs):
        self.groups = mesh.shape["seq"] // seqs
        self.seqs = seqs

    def place(self):
        me = lax.axis_index("seq")
        return me // self.groups, me % self.groups

    def fetch(self, tokens, triple, small, merger, widener, narrower):
        both = ("batch", "seq")
        seq, group = self.place()
        wide = triple.shape[2] // self.groups
        rows = lax.all_gather(tokens, "seq", axis=1, tiled=True)
        rows = lax.dynamic_index_in_dim(rows, seq, 0, keepdims=False)
        triple = lax.all_gather(triple, both, axis=1, tiled=True)
        triple = lax.dynamic_slice_in_dim(triple, group * wide, wide, 2)
        return (
            rows,
            triple,
            lax.all_gather(small, both, axis=0, tiled=False),
            lax.all_gather(merger, both, axis=0, tiled=True),
            lax.all_gather(widener, both, axis=0, tiled=True),
            lax.all_gather(narrower, both, axis=0, tiled=True),
        )

    def to_rows(self, part):
        count = self.seqs * self.groups
        length, wide = part.shape
        parts = lax.all_to_all(part.reshape(count, length // count, wide), "seq", 0, 0)
        parts = parts.reshape(self.seqs, self.groups, length // count, wide)
        return jnp.transpose(parts, (0, 2, 1, 3)).reshape(-1, self.groups * wide)

    def to_groups(self, rows):
        count = self.seqs * self.groups
        parts = rows.reshape(self.seqs, -1, self.groups, rows.shape[1] // self.groups)
        parts = jnp.transpose(parts, (0, 2, 1, 3)).reshape(count, parts.shape[1], parts.shape[3])
        parts = lax.all_to_all(parts, "seq", 0, 0)
        return parts.reshape(-1, parts.shape[2])

    def settle(self, part, triple, small, merger, widener, narrower):
        both = ("batch", "seq")
        seq, group = self.place()
        length, width = part.shape
        rows = jnp.zeros((self.seqs, length, width), part.dtype)
        rows = lax.dynamic_update_index_in_dim(rows, part, seq, 0)
        rows = lax.psum_scatter(rows, "seq", scatter_dimension=1, tiled=True)
        full = jnp.zeros(triple.shape[:2] + (triple.shape[2] * self.groups,), triple.dtype)
        full = lax.dynamic_update_slice_in_dim(full, triple, group * triple.shape[2], 2)
        return (
            rows.reshape(-1, width),
            lax.psum_scatter(full, both, scatter_dimension=1, tiled=True),
            lax.psum_scatter(small, both, scatter_dimension=0, tiled=False),
            lax.psum_scatter(merger, both, scatter_dimension=0, tiled=True),
            lax.psum_scatter(widener, both, scatter_dimension=0, tiled=True),
            lax.psum_scatter(narrower, both, scatter_dimension=0, tiled=True),
        )


def on_device(
    links, tokens, segments, qkv_weight, qv_bias, attn_out_weight, attn_out_bias, norm1_gain,
    norm1_bias, up_weight, up_bias, down_weight, down_bias, norm2_gain, norm2_bias, cotangent,
):
    seqs, rows, width = tokens.shape
    piece = attn_out_bias.shape[0]
    ratio = up_bias.shape[0] // piece
    block = 256
    seq, group = links.place()
    wide = width // links.groups
    small = jnp.concatenate(
        [qv_bias, jnp.stack([attn_out_bias, norm1_gain, norm1_bias, down_bias, norm2_gain, norm2_bias]),
         up_bias.reshape(ratio, piece)], axis=0,
    )
    full, triple, small, merger, widener, narrower = links.fetch(
        tokens, qkv_weight.astype(BF16), small.astype(BF16),
        attn_out_weight.astype(BF16), up_weight.astype(BF16), down_weight.astype(BF16),
    )
    vectors = spread(small[:, :8]).astype(F32)
    wide_bias = small[:, 8:].reshape(1, -1).astype(F32)
    biases = lax.dynamic_slice_in_dim(vectors[:2], group * wide, wide, 1)
    biases = jnp.stack([biases[0], jnp.zeros_like(biases[0]), biases[1]])
    docs = lax.dynamic_index_in_dim(segments, seq, 0, keepdims=False)
    low, high = block_ranges(docs, block)
    query, key, value, context, turned, log = attend(full, triple, biases, docs, low, high, block)
    output, grad_context, grad_mid, grad_merger, grad_widener, grad_narrower, sums, wide_sum = dense(
        links.to_rows(context), tokens.reshape(-1, width), cotangent.reshape(-1, width),
        vectors[2:], wide_bias, merger, widener, narrower,
    )
    part, grad_triple, bias_sums = attend_back(
        full, triple, docs, low, high, query, key, value, turned, log,
        links.to_groups(grad_context), block,
    )
    bias_full = jnp.zeros((2, width), F32)
    bias_full = lax.dynamic_update_slice_in_dim(bias_full, bias_sums, group * wide, 1)
    owners = width // piece
    small_sums = jnp.concatenate([bias_full, sums[:6]], axis=0).reshape(8, owners, piece)
    small_sums = jnp.concatenate(
        [jnp.transpose(small_sums, (1, 0, 2)), wide_sum.reshape(owners, ratio, piece)], axis=1
    )
    grad_rows, grad_triple, small_sums, grad_merger, grad_widener, grad_narrower = links.settle(
        part, grad_triple, small_sums, grad_merger, grad_widener, grad_narrower
    )
    grad_rows = (grad_rows.astype(F32) + grad_mid).astype(BF16)
    return (
        output.reshape(tokens.shape),
        grad_rows.reshape(tokens.shape),
        grad_triple.astype(F32),
        small_sums[:2],
        grad_merger.astype(F32),
        small_sums[2],
        small_sums[3],
        small_sums[4],
        grad_widener.astype(F32),
        small_sums[8:].reshape(-1),
        grad_narrower.astype(F32),
        small_sums[5],
        small_sums[6],
        small_sums[7],
    )


def solution(mesh):
    both = ("batch", "seq")
    token = P("batch", "seq", None)
    matrix = P(both, None)
    vector = P(both)
    weights = (
        P(None, both, None), P(None, both), matrix, vector, vector, vector,
        matrix, vector, matrix, vector, vector, vector,
    )

    def program(tokens, *rest):
        links = PlainLinks(mesh, tokens.shape[0])
        return on_device(links, tokens, *rest)

    return jax.shard_map(
        program,
        mesh=mesh,
        in_specs=(token, P("batch", None)) + weights + (token,),
        out_specs=(token, token) + weights,
        check_vma=False,
    )
```

time: 1200 us -> 828 us (0.69)
  matrix products: 226 us -> 0 us
  waiting for transfers between devices: 676 us -> 503 us
  Pallas kernels: 0 us -> 126 us
  local copies, waits for them, and re-layouts: 83.6 us -> 35.4 us
  other arithmetic: 37.7 us -> 15 us
  blocking collectives: 149 us -> 129 us
    dot_general x40 -> x0, matrix products: 226 us -> none  [the longest x8 43.7 us: masked_scores(): jnp.einsum('sqhd,skhd->shqk', queries, key_rows, preferred_element_type=j...]
    reduce_scatter x4, waiting for transfers between devices: 454 us -> 265 us  [the longest x1 110 us: settle(): lax.psum_scatter(widener, both, scatter_dimension=0, tiled=True)]
    pallas_call x0 -> x3, Pallas kernels: none -> 126 us  [the longest x1 57.2 us: attend_back(): pl.pallas_call(functools.partial(attend_back_kernel, heads, block), out_s...]
    all_gather x6 -> x5, waiting for transfers between devices: 104 us -> 166 us  [the longest x1 65.5 us: fetch(): lax.all_gather(widener, both, axis=0, tiled=True)]
    unnamed x12 -> x11, waiting for transfers between devices: 119 us -> 60.8 us
    unnamed x2 -> x1, blocking collectives: 79.4 us -> 43.8 us
    unnamed x131 -> x38, local copies, waits for them, and re-layouts: 28.1 us -> 8.41 us
    reduce_sum x14 -> x1, other arithmetic: 18.9 us -> 0.22 us  [block_ranges(): high = jnp.sum((docs[None, :] <= grouped[:, -1:]).astype(jnp.int32), axis=1)]
  transfers between devices with their start and end apart: 11 -> 11, of which waited for: 8 -> 9; matrix products, arithmetic and copies ran while one was open for 13% -> 5% of each run, Pallas kernels for 0% -> 11%
where the time goes in v1:
time: 828 us; the launch traced here: 827 us
  waiting for transfers between devices  503 us (61%)
  blocking collectives  129 us (16%)
  Pallas kernels  126 us (15%)
  local copies, waits for them, and re-layouts  35.4 us (4%)
  other arithmetic  15 us (2%)
  between operations  14.6 us (2%)
    reduce_scatter x1, waiting for transfers between devices, settle(): lax.psum_scatter(widener, both, scatter_dimension=0, tiled=True)  110 us
    reduce_scatter x1, waiting for transfers between devices, settle(): lax.psum_scatter(narrower, both, scatter_dimension=0, tiled=True)  110 us
    all_gather x1, blocking collectives, fetch(): lax.all_gather(small, both, axis=0, tiled=False)  70.7 us
    all_gather x1, waiting for transfers between devices, fetch(): lax.all_gather(widener, both, axis=0, tiled=True)  65.5 us
    all_gather x1, waiting for transfers between devices, fetch(): lax.all_gather(narrower, both, axis=0, tiled=True)  65.2 us
    unnamed x11, waiting for transfers between devices  60.8 us
    pallas_call x1, Pallas kernels, attend_back(): pl.pallas_call(functools.partial(attend_back_kernel, heads, block), out_s...  57.2 us
    reduce_scatter x1, waiting for transfers between devices, settle(): rows = lax.psum_scatter(rows, 'seq', scatter_dimension=1, tiled=True)  44.1 us
  transfers between devices with their start and end apart: 11, of which 9 were waited for; matrix products, arithmetic and copies ran while one was open for 5% of the time, Pallas kernels for 11%

profile of v1, /device:TPU:0, one launch (start us, length us, event | category | flops | bytes accessed | tf_op | source)
XLA Modules:
  0.0 826.7 jit_solution(13890573327402371605)
XLA Ops:
  7.3 1.7 convert_element_type.61
  9.1 0.7 all-gather.6.cloned.1.call-update
  9.9 1.5 convert_element_type.66
  11.5 0.7 convert_element_type.67
  12.2 0.7 convert_element_type.68
  13.2 70.7 %all_gather.21 = bf16[32,12,24]{2,1,0:T(8,128)(2,1)S(1)} all-gather(bf16[1,12,24]{2,1,0:T(8,128)(2,1)S(1)} %concatenate.41), channel_id=1, replica_groups=mesh['batch'=8,'seq'=4] {'batch','seq'}, dimensions={0}, use_global_device_ids=true | all-gather | bytes 19008 | tf_op jit(solution)/shard_map/all_gather | solution.py:447
  84.0 0.5 broadcast.43
  84.6 0.7 reduce.10
  85.9 0.5 and_select_fusion
  86.4 0.7 pad_maximum_fusion.2.bias_ref
  87.1 3.0 constant_dynamic-slice_fusion.8.weight_ref
  90.1 29.1 %all-gather.6.cloned.1.call-done = bf16[1,2048,768]{2,1,0:T(8,128)(2,1)} async-done(((bf16[1,512,768]{2,1,0:T(8,128)(2,1)}), bf16[1,2048,768]{2,1,0:T(8,128)(2,1)}) %all-gather.6.cloned.1.call-update) | async-done | bytes 3145744 | tf_op jit(solution)/shard_map/all_gather | solution.py:440
  119.2 33.6 %attend.1 = (bf16[3,2048,64]{2,1,0:T(8,128)(2,1)}, bf16[3,2048,64]{2,1,0:T(8,128)(2,1)}, bf16[3,2048,64]{2,1,0:T(8,128)(2,1)}, bf16[2048,192]{1,0:T(8,128)(2,1)}...) custom-call(s32[8]{0:T(128)} %get-tuple-element.61.low_ref, s32[8]{0:T(128)} %get-tuple-element.60.high_ref, ...), custom_call_target="tpu_custom_call" | custom-call | tf_op jit(solution)/shard_map/attend/pallas_call | solution.py:118
  152.8 2.2 copy.57
  155.0 3.5 all-to-all-start
  158.6 0.7 slice.75.vector_ref
  159.4 0.7 reshape.247.wide_ref
  160.1 11.5 %all-to-all-done = bf16[4,512,192]{1,2,0:T(8,128)(2,1)S(1)} async-done(((bf16[4,512,192]{1,2,0:T(8,128)(2,1)}), bf16[4,512,192]{1,2,0:T(8,128)(2,1)S(1)}, u32[]{:S(2)}, u32[]{:S(2)}) %all-to-all-start) | async-done | bytes 786464 | tf_op jit(solution)/shard_map/all_to_all | solution.py:456
  171.6 1.2 copy.59.context_ref
  172.7 6.3 all-gather.10.cloned.1.call-done.merger_hbm
  179.0 65.5 %all-gather.12.cloned.1.call-done.widener_hbm = bf16[768,3072]{1,0:T(8,128)(2,1)} async-done(((bf16[24,3072]{1,0:T(8,128)(2,1)}), bf16[768,3072]{1,0:T(8,128)(2,1)}) %all-gather.12.cloned.1.call-update) | async-done | bytes 4718608 | tf_op jit(solution)/shard_map/all_gather | solution.py:449
  244.5 65.2 %all-gather.14.cloned.1.call-done.narrower_hbm = bf16[3072,768]{1,0:T(8,128)(2,1)} async-done(((bf16[96,768]{1,0:T(8,128)(2,1)}), bf16[3072,768]{1,0:T(8,128)(2,1)}) %all-gather.14.cloned.1.call-update) | async-done | bytes 4718608 | tf_op jit(solution)/shard_map/all_gather | solution.py:450
  309.6 35.0 %dense.1 = (bf16[512,768]{1,0:T(8,128)(2,1)}, bf16[512,768]{1,0:T(8,128)(2,1)}, f32[512,768]{1,0:T(8,128)}, bf16[768,768]{1,0:T(8,128)(2,1)}, bf16[768,3072]{1,0...) custom-call(bf16[512,768]{1,0:T(8,128)(2,1)} %copy.59.context_ref, ...), custom_call_target="tpu_custom_call" | custom-call | tf_op jit(solution)/shard_map/dense/pallas_call | solution.py:382
  344.7 1.1 copy-done.1
  346.0 14.4 %all_to_all.10 = bf16[4,512,192]{1,2,0:T(8,128)(2,1)S(1)} all-to-all(bf16[4,512,192]{1,2,0:T(8,128)(2,1)S(1)} %bitcast.69), channel_id=1, replica_groups=mesh['batch'=8,'seq'=4] {'seq'}, dimensions={0} | all-to-all | bytes 1572864 | tf_op jit(solution)/shard_map/all_to_all | solution.py:464
  360.5 1.3 copy.61
  361.8 57.2 %attend_back.1 = (bf16[2048,768]{1,0:T(8,128)(2,1)}, bf16[3,768,192]{2,1,0:T(8,128)(2,1)}, f32[2,192]{1,0:T(2,128)}) custom-call(s32[8]{0:T(128)} %get-tuple-element.61.low_ref, s32[8]{0:T(128)} %get-tuple-element.60.high_ref, bf16[2048,768]{1,0:T(8,128)(2,1)} %bitcast.64, bf16[3,768,192]{2,1,0:T(8,128)(2,1)} %constant_dynamic-slice_fusion.8.weight_ref, ...), custom_call_target="tpu_custom_call" | custom-call | tf_op jit(solution)/shard_map/attend_back/pallas_call | solution.py:235
  419.2 14.2 %dynamic_update_slice.8 = bf16[3,768,768]{2,1,0:T(8,128)(2,1)S(1)} dynamic-update-slice(bf16[3,768,768]{2,1,0:T(8,128)(2,1)S(1)} %broadcast_in_dim.14, bf16[3,768,192]{2,1,0:T(8,128)(2,1)} %get-tuple-element.41, s32[]{:T(128)} %constant.70.clone.1, s32[]{:T(128)} %constant.70.clone.1, s32[]{:T(128)S(6)} %select_n.38) | dynamic-update-slice | bytes 1769476 | tf_op jit(solution)/shard_map/dynamic_update_slice | solution.py:475
  433.4 3.0 copy.63
  436.4 2.6 copy.69
  439.1 0.7 reduce-scatter.13.cloned.1.call-update
  439.9 0.7 reduce-scatter.15.cloned.1.call-update
  441.2 0.5 broadcast.44
  441.7 0.7 reduce.11
  442.9 43.8 %all-reduce = f32[32,12,24]{2,0,1:T(8,128)S(1)} all-reduce(f32[32,12,24]{2,0,1:T(8,128)S(1)} %pad_maximum_fusion), channel_id=4, replica_groups=mesh['batch'=8,'seq'=4] {'batch','seq'}, use_global_device_ids=true, to_apply=%region_4.5.clone | all-reduce | flops 9216 | bytes 73728
  486.7 0.6 reshape.246
  487.3 0.6 constant_dynamic-slice_fusion.5
  487.9 0.5 fusion.2
  488.4 1.4 convert_element_type.73
  489.8 58.2 %reduce-scatter.17.cloned.1.call-done = bf16[24,2304]{1,0:T(8,128)(2,1)} async-done(((bf16[768,2304]{1,0:T(8,128)(2,1)}), bf16[24,2304]{1,0:T(8,128)(2,1)}) %reduce-scatter.17.cloned.1.call-update) | async-done | bytes 110608
  548.0 0.9 reshape.250
  549.0 0.7 copy_convert_fusion
  549.7 110.3 %reduce-scatter.13.cloned.1.call-done = bf16[24,3072]{1,0:T(8,128)(2,1)} async-done(((bf16[768,3072]{1,0:T(8,128)(2,1)}), bf16[24,3072]{1,0:T(8,128)(2,1)}) %reduce-scatter.13.cloned.1.call-update) | async-done | bytes 147472 | tf_op jit(solution)/shard_map/reduce_scatter | solution.py:481
  660.0 1.6 convert_element_type.74
  661.7 110.3 %reduce-scatter.15.cloned.1.call-done = bf16[96,768]{1,0:T(8,128)(2,1)} async-done(((bf16[3072,768]{1,0:T(8,128)(2,1)}), bf16[96,768]{1,0:T(8,128)(2,1)}) %reduce-scatter.15.cloned.1.call-update) | async-done | bytes 147472 | tf_op jit(solution)/shard_map/reduce_scatter | solution.py:482
  772.0 1.6 convert_element_type.75
  773.6 44.1 %reduce-scatter.9.cloned.1.call-done = bf16[1,512,768]{2,1,0:T(8,128)(2,1)} async-done(((bf16[1,2048,768]{2,1,0:T(8,128)(2,1)}), bf16[1,512,768]{2,1,0:T(8,128)(2,1)}) %reduce-scatter.9.cloned.1.call-update) | async-done | bytes 786448 | tf_op jit(solution)/shard_map/reduce_scatter | solution.py:473
  817.7 2.2 fusion.1
  (81 shorter events, 3.0 us)
Async XLA Ops:
  7.2 4.3 copy-start.2
  7.2 5.0 copy-start.3
  7.2 5.8 copy-start.15
  7.2 5.8 copy-start.14
  7.2 5.8 copy-start.9
  7.2 5.8 copy-start.8
  7.2 5.9 copy-start.11
  7.3 5.9 copy-start.10
  7.3 5.9 copy-start.13
  7.3 5.9 copy-start.12
  7.3 77.3 %copy-start.4 = (s32[1,2048]{1,0:T(1,128)S(1)}, s32[1,2048]{1,0:T(1,128)}, u32[]{:S(2)}) copy-start(s32[1,2048]{1,0:T(1,128)} %doc_row_ref.1) | copy-start | bytes 24580
  7.3 79.8 %all-gather.8.cloned.1.call-start = ((), (), s32[]{:S(2)}) async-start(), calls=%async_computation.8 | async-start | bytes 3649536 | tf_op jit(solution)/shard_map/all_gather | solution.py:442
  9.1 110.1 %all-gather.6.cloned.1.call-start = ((), (), s32[]{:S(2)}) async-start(), calls=%async_computation.7 | async-start | bytes 3932160 | tf_op jit(solution)/shard_map/all_gather | solution.py:440
  9.8 169.2 %all-gather.10.cloned.1.call-start = ((), (), s32[]{:S(2)}) async-start(), calls=%async_computation.9 | async-start | bytes 1216512 | tf_op jit(solution)/shard_map/all_gather | solution.py:448
  11.4 233.0 %all-gather.12.cloned.1.call-start = ((), (), s32[]{:S(2)}) async-start(), calls=%async_computation.10 | async-start | bytes 4866048 | tf_op jit(solution)/shard_map/all_gather | solution.py:449
  12.2 297.4 %all-gather.14.cloned.1.call-start = ((), (), s32[]{:S(2)}) async-start(), calls=%async_computation.11 | async-start | bytes 4866048 | tf_op jit(solution)/shard_map/all_gather | solution.py:450
  155.0 16.5 %all-to-all-start = ((bf16[4,512,192]{1,2,0:T(8,128)(2,1)}), bf16[4,512,192]{1,2,0:T(8,128)(2,1)S(1)}, u32[]{:S(2)}, u32[]{:S(2)}) async-start(bf16[4,512,192]{1,2,0:T(8,128)(2,1)} %copy.57), calls=%async_computation | async-start | bytes 1572864 | tf_op jit(solution)/shard_map/all_to_all | solution.py:456
  158.5 329.9 %reduce-scatter.11.cloned.1.call-start = ((), (), s32[]{:S(2)}) async-start(), calls=%async_computation.13 | async-start | bytes 1216512 | tf_op jit(solution)/shard_map/reduce_scatter | solution.py:480
  344.6 1.1 copy-start.1
  344.6 203.4 %reduce-scatter.17.cloned.1.call-start = ((), (), s32[]{:S(2)}) async-start(), calls=%async_computation.16 | async-start | bytes 3649536
  439.1 221.0 %reduce-scatter.13.cloned.1.call-start = ((), (), s32[]{:S(2)}) async-start(), calls=%async_computation.14 | async-start | bytes 4866048 | tf_op jit(solution)/shard_map/reduce_scatter | solution.py:481
  439.8 332.2 %reduce-scatter.15.cloned.1.call-start = ((), (), s32[]{:S(2)}) async-start(), calls=%async_computation.15 | async-start | bytes 4866048 | tf_op jit(solution)/shard_map/reduce_scatter | solution.py:482
  440.6 377.2 %reduce-scatter.9.cloned.1.call-start = ((), (), s32[]{:S(2)}) async-start(), calls=%async_computation.12 | async-start | bytes 3932160 | tf_op jit(solution)/shard_map/reduce_scatter | solution.py:473
  440.6 1.1 copy-start.6
  440.6 1.9 copy-start.7
  440.6 2.1 copy-start.5
  441.1 376.6 %copy-start = (f32[512,768]{1,0:T(8,128)S(1)}, f32[512,768]{1,0:T(8,128)}, u32[]{:S(2)}) copy-start(f32[512,768]{1,0:T(8,128)} %get-tuple-element.40) | copy-start | bytes 4718596
Sparse Core Ops, SparseCore 0:
  11.5 63.1 all-gather.7
  76.5 42.6 all-gather.5
  122.7 56.2 all-gather.9
  182.3 62.0 all-gather.11
  247.8 61.8 all-gather.13
  344.7 95.3 reduce-scatter.10
  445.6 102.3 reduce-scatter.16
  553.5 106.4 reduce-scatter.12
  665.5 106.4 reduce-scatter.14
  774.8 42.8 reduce-scatter.8
